TPU v7x, 512 devices: a whole 4x8x8 slice. The times are simulated.
512 devices in a mesh: pipe: 8 (over y_lo, core), tensor: 64 (over y_hi, x, z).
Axes of the slice: x: 4, y: 8 (y_hi: 2, y_lo: 4; y = y_hi * 4 + y_lo), z: 8, core: 2. Of those that a mesh axis runs over, the one named last changes fastest.
Arguments:
- output_gradient: bfloat16 [8, 64, 2, 64, 1024], P('pipe', 'tensor'), may hold values from -6 to 6
- forward_input: bfloat16 [8, 2, 512, 8192], P('pipe', None, None, 'tensor'), may hold values from -6 to 6
- saved_rank_outputs: bfloat16 [8, 2, 512, 64], P('pipe', None, 'tensor'), may hold values from -6 to 6
- projection_weight: bfloat16 [8, 64, 1024, 1024], P('pipe', 'tensor'), may hold values from -0.0625 to 0.0625
- adapter_down_maps: bfloat16 [8, 8, 64, 8192], P('pipe', None, None, 'tensor'), may hold values from -0.75 to 0.75
- adapter_up_maps: bfloat16 [8, 64, 8, 8, 1024], P('pipe', 'tensor'), may hold values from -0.0625 to 0.0625
- segment_adapter_class: int32 [8, 2, 4], P('pipe'), may hold values from 0 to 7
- live_segment_table: int32 [8, 2], P('pipe'), may hold values from 1 to 4, as said below
Outputs:
- grad_prev: bfloat16 [8, 2, 512, 8192], P('pipe', None, None, 'tensor')
- down_map_gradient: bfloat16 [8, 8, 64, 8192], P('pipe', None, None, 'tensor')
- up_map_gradient: bfloat16 [8, 64, 8, 8, 1024], P('pipe', 'tensor')
Inputs may be any that keep to these rules, and one draw needn't show every extreme that they name: The first live_segment_table segments of a microbatch are live; some microbatch has all 4 live.
All inputs are finite; a program needn't handle non-finite values.
Results may differ from a plain program's by a relative error of at most 0.0049.
Values may be sent and summed in bfloat16 or wider, within the bound.
A program may use at most 64 MiB of HBM per device.

v0:
```python
import jax
import jax.numpy as jnp
from jax import lax
from jax.sharding import PartitionSpec as P

SEG = 128


def partner(value, axis, apart):
    mask = 2**apart
    pairs = [(source, source ^ mask) for source in range(lax.axis_size(axis))]
    return lax.ppermute(value, axis, pairs)


def shifted(block, axis, distance):
    devices = range(lax.axis_size(axis))
    route = [((i - distance) % len(devices), i) for i in devices]
    return lax.ppermute(block, axis, route)


def choose_segment_rows(class_indicator, segment_lookup):
    return jnp.einsum(
        "pzw,wlq->pzlq", class_indicator, segment_lookup, preferred_element_type=jnp.float32
    ).astype(jnp.bfloat16)


def shards(
    output_gradient,
    forward_input,
    saved_rank_outputs,
    projection_weight,
    adapter_down_maps,
    adapter_up_maps,
    segment_adapter_class,
    live_segment_table,
):
    grad_tile = output_gradient[0, 0]
    micro_count, tile_rows, tile_cols = grad_tile.shape
    weight = projection_weight[0, 0]
    up_matrix_tile = adapter_up_maps[0, 0]
    rank_part = up_matrix_tile.shape[1]
    rank_extent = adapter_down_maps.shape[2]
    local_portion = adapter_down_maps.shape[3]
    group_size = lax.axis_size("tensor")
    total_bits = group_size.bit_length() - 1
    low_size = min(group_size, 8)
    low_bits = low_size.bit_length() - 1
    high_size = group_size // low_size
    position = lax.axis_index("tensor")
    high_index = position // low_size
    batch_rows = tile_rows * high_size
    seg_count = batch_rows // SEG
    row_ids = high_index * tile_rows + jnp.arange(tile_rows, dtype=jnp.int32)
    live_count = live_segment_table[0]
    keep_rows = (row_ids // SEG)[None, :] < live_count[:, None]
    masked_tile = jnp.where(keep_rows[:, :, None], grad_tile, jnp.zeros_like(grad_tile))
    gathered = masked_tile
    for level in range(low_bits, total_bits):
        received = partner(gathered, "tensor", level)
        leading = position >> level & 1 == 0
        gathered = jnp.where(
            leading,
            jnp.concatenate([gathered, received], 1),
            jnp.concatenate([received, gathered], 1),
        )
    products = jnp.einsum("mrd,id->mri", gathered, weight, preferred_element_type=jnp.float32)
    reduced = products
    for level in reversed(range(low_bits)):
        half_cols = reduced.shape[2] // 2
        lower_half = reduced[:, :, :half_cols]
        upper_half = reduced[:, :, half_cols:]
        upper_side = position >> level & 1 == 1
        kept_half = jnp.where(upper_side, upper_half, lower_half)
        sent_half = jnp.where(upper_side, lower_half, upper_half)
        reduced = kept_half + partner(sent_half, "tensor", level)
    classes = segment_adapter_class[0]
    class_indicator = (
        classes[:, :, None] == jnp.arange(up_matrix_tile.shape[0], dtype=jnp.int32)[None, None, :]
    ).astype(jnp.bfloat16)
    selected_up_matrix = choose_segment_rows(class_indicator, up_matrix_tile)
    grad_segs = gathered.reshape(micro_count, seg_count, SEG, tile_cols)
    partial_rank = jnp.einsum(
        "mskd,msrd->mskr", grad_segs, selected_up_matrix, preferred_element_type=jnp.float32
    )
    padded_rank = jnp.zeros((micro_count, seg_count, SEG, rank_extent), jnp.float32)
    padded_rank = lax.dynamic_update_slice_in_dim(
        padded_rank, partial_rank, high_index * rank_part, 3
    )
    lowrank = lax.psum(padded_rank, "tensor").astype(jnp.bfloat16)
    selected_down_matrix = choose_segment_rows(class_indicator, adapter_down_maps[0])
    adapter = jnp.einsum(
        "mskr,msrd->mskd", lowrank, selected_down_matrix, preferred_element_type=jnp.float32
    )
    input_gradient = (reduced + adapter.reshape(micro_count, batch_rows, local_portion)).astype(
        jnp.bfloat16
    )
    grad_prev = shifted(input_gradient, "pipe", -1)
    inputs_seg = forward_input[0].reshape(micro_count, seg_count, SEG, local_portion)
    segment_down_matrix = jnp.einsum(
        "mskr,mskd->msrd", lowrank, inputs_seg, preferred_element_type=jnp.float32
    )
    hidden = lax.all_gather(saved_rank_outputs[0], "tensor", axis=1, tiled=True)
    hidden_part = lax.dynamic_slice_in_dim(hidden, high_index * rank_part, rank_part, 2)
    hidden_seg = hidden_part.reshape(micro_count, seg_count, SEG, rank_part)
    segment_up_matrix = jnp.einsum(
        "mskr,mskd->msrd", hidden_seg, grad_segs, preferred_element_type=jnp.float32
    )
    wide_class_indicator = class_indicator.astype(jnp.float32)
    down_map_gradient = jnp.einsum(
        "exk,exlq->klq", wide_class_indicator, segment_down_matrix, precision=lax.Precision.HIGHEST
    ).astype(jnp.bfloat16)
    up_map_gradient = jnp.einsum(
        "exk,exlq->klq", wide_class_indicator, segment_up_matrix, precision=lax.Precision.HIGHEST
    ).astype(jnp.bfloat16)
    return (grad_prev[None], down_map_gradient[None], up_map_gradient[None, None])


def solution(mesh):
    in_specs = (
        P("pipe", "tensor", None, None, None),
        P("pipe", None, None, "tensor"),
        P("pipe", None, "tensor", None),
        P("pipe", "tensor", None, None),
        P("pipe", None, None, "tensor"),
        P("pipe", "tensor", None, None, None),
        P("pipe", None, None),
        P("pipe", None),
    )
    out_specs = (
        P("pipe", None, None, "tensor"),
        P("pipe", None, None, "tensor"),
        P("pipe", "tensor", None, None, None),
    )
    return jax.shard_map(shards, mesh=mesh, in_specs=in_specs, out_specs=out_specs, check_vma=False)
```

profile of v0, /device:TPU:9, one launch (start us, length us, event | category | flops | bytes accessed | tf_op | source)
XLA Modules:
  0.0 877.9 jit_solution(1295151885727014478)
XLA Ops:
  2.6 3.1 collective-permute-start
  5.7 6.0 collective-permute-done
  11.8 4.7 collective-permute-start.1
  16.5 10.8 %collective-permute-done.1 = bf16[2,128,1024]{2,1,0:T(8,128)(2,1)} collective-permute-done((bf16[2,128,1024]{2,1,0:T(8,128)(2,1)S(1)}, bf16[2,128,1024]{2,1,0:T(8,128)(2,1)}, u32[]{:S(2)}, u32[]{:S(2)}) %collective-permute-start.1) | collective-permute-done | bytes 524320 | tf_op jit(solution)/shard_map/ppermute | solution.py:12
  27.3 2.1 maximum_select_fusion.1
  29.4 6.6 collective-permute-start.2
  35.9 43.0 %collective-permute-done.2 = bf16[2,256,1024]{2,1,0:T(8,128)(2,1)} collective-permute-done((bf16[2,256,1024]{2,1,0:T(8,128)(2,1)S(1)}, bf16[2,256,1024]{2,1,0:T(8,128)(2,1)}, u32[]{:S(2)}, u32[]{:S(2)}) %collective-permute-start.2) | collective-permute-done | bytes 1048608 | tf_op jit(solution)/shard_map/ppermute | solution.py:12
  78.9 2.6 maximum_select_fusion
  81.5 2.4 fusion
  83.9 2.2 slice_select_fusion
  86.7 10.6 %collective-permute-start.3 = (f32[2,512,512]{2,1,0:T(8,128)}, f32[2,512,512]{2,1,0:T(8,128)}, u32[]{:S(2)}, u32[]{:S(2)}) collective-permute-start(f32[2,512,512]{2,1,0:T(8,128)} %slice_select_fusion), channel_id=1, source_target_pairs={{0,4},{1,5},{2,6},{3,7},{4,0},{5,1},{6,2},{7,3},{8,12},{9,13},{10,... | collective-permute-start | bytes 6291464 | tf_op jit(solution)/shard_map/ppermute | solution.py:12
  97.3 272.6 %all-gather = bf16[1,2,512,64]{3,2,1,0:T(8,128)(2,1)S(1)} all-gather(bf16[1,2,8,64]{3,2,1,0:T(8,128)(2,1)S(1)} %copy-done.12), channel_id=2, replica_groups=mesh['pipe'=8,'tensor'=64] {'tensor'}, dimensions={2}, use_global_device_ids=true | all-gather | bytes 133120 | tf_op jit(solution)/shard_map/all_gather | solution.py:102
  370.0 3.6 select_add_fusion
  373.6 1.3 copy-done.3
  375.1 1.9 collective-permute-start.4
  379.3 2.4 convolution_dynamic-update-slice_fusion
  382.8 14.4 %collective-permute-done.4 = f32[2,512,256]{2,1,0:T(8,128)} collective-permute-done((f32[2,512,256]{2,1,0:T(8,128)S(1)}, f32[2,512,256]{2,1,0:T(8,128)}, u32[]{:S(2)}, u32[]{:S(2)}) %collective-permute-start.4) | collective-permute-done | bytes 1048608 | tf_op jit(solution)/shard_map/ppermute | solution.py:12
  397.2 1.4 select_add_fusion.1
  399.4 1.9 collective-permute-start.5
  402.7 374.2 %all-reduce.1 = bf16[2,4,128,64]{2,3,1,0:T(8,128)(2,1)S(1)} all-reduce(f32[2,4,128,64]{2,3,1,0:T(8,128)S(1)} %copy-done.8), channel_id=1, replica_groups=mesh['pipe'=8,'tensor'=64] {'tensor'}, use_global_device_ids=true, to_apply=%region_0.1 | all-reduce | flops 65536 | bytes 393216 | tf_op jit(solution)/shard_map/psum | solution.py:89
  776.9 1.2 fusion.9
  778.1 1.2 fusion.6
  779.3 90.0 %collective-permute-start.6 = (bf16[2,512,128]{2,1,0:T(8,128)(2,1)S(1)}, bf16[2,512,128]{2,1,0:T(8,128)(2,1)S(1)}, u32[]{:S(2)}, u32[]{:S(2)}) collective-permute-start(bf16[2,512,128]{2,1,0:T(8,128)(2,1)S(1)} %fusion.6), channel_id=1, source_target_pairs={{64,0},{128,64},{192,128},{256,192},{320,256},{384,320},{448,384},... | collective-permute-start | bytes 786440 | tf_op jit(solution)/shard_map/ppermute | solution.py:18
  870.8 6.4 collective-permute-done.6
  (44 shorter events, 10.4 us)
Async XLA Ops:
  0.6 80.9 %copy-start = (bf16[1,1,1024,1024]{3,2,1,0:T(8,128)(2,1)S(1)}, bf16[1,1,1024,1024]{3,2,1,0:T(8,128)(2,1)}, u32[]{:S(2)}) copy-start(bf16[1,1,1024,1024]{3,2,1,0:T(8,128)(2,1)} %param.11) | copy-start | bytes 6291460
  2.6 9.1 %collective-permute-start = (bf16[2,64,1024]{2,1,0:T(8,128)(2,1)S(1)}, bf16[2,64,1024]{2,1,0:T(8,128)(2,1)S(1)}, u32[]{:S(2)}, u32[]{:S(2)}) collective-permute-start(bf16[2,64,1024]{2,1,0:T(8,128)(2,1)S(1)} %bitcast_select_fusion), channel_id=1, source_target_pairs={{0,8},{1,9},{2,10},{3,11},{4,12},{5,13},{6,14},{7,15},{8,0},{9,1},... | collective-permute-start | bytes 786440 | tf_op jit(solution)/shard_map/ppermute | solution.py:12
  11.8 4.7 copy-start.6
  11.8 15.5 %collective-permute-start.1 = (bf16[2,128,1024]{2,1,0:T(8,128)(2,1)S(1)}, bf16[2,128,1024]{2,1,0:T(8,128)(2,1)}, u32[]{:S(2)}, u32[]{:S(2)}) collective-permute-start(bf16[2,128,1024]{2,1,0:T(8,128)(2,1)S(1)} %maximum_select_fusion.2), channel_id=1, source_target_pairs={{0,16},{1,17},{2,18},{3,19},{4,20},{5,21},{6,22},{7,23},{8,24},{9,... | collective-permute-start | bytes 1572872 | tf_op jit(solution)/shard_map/ppermute | solution.py:12
  29.4 49.6 %collective-permute-start.2 = (bf16[2,256,1024]{2,1,0:T(8,128)(2,1)S(1)}, bf16[2,256,1024]{2,1,0:T(8,128)(2,1)}, u32[]{:S(2)}, u32[]{:S(2)}) collective-permute-start(bf16[2,256,1024]{2,1,0:T(8,128)(2,1)S(1)} %maximum_select_fusion.1), channel_id=1, source_target_pairs={{0,32},{1,33},{2,34},{3,35},{4,36},{5,37},{6,38},{7,39},{8,40},{9,... | collective-permute-start | bytes 3145736 | tf_op jit(solution)/shard_map/ppermute | solution.py:12
  81.5 2.4 copy-start.1
  83.9 2.7 copy-start.5
  83.9 13.4 %copy-start.12 = (bf16[1,2,8,64]{3,2,1,0:T(8,128)(2,1)S(1)}, bf16[1,2,8,64]{3,2,1,0:T(8,128)(2,1)}, u32[]{:S(2)}) copy-start(bf16[1,2,8,64]{3,2,1,0:T(8,128)(2,1)} %param.10) | copy-start | bytes 6148
  86.7 283.3 %collective-permute-start.3 = (f32[2,512,512]{2,1,0:T(8,128)}, f32[2,512,512]{2,1,0:T(8,128)}, u32[]{:S(2)}, u32[]{:S(2)}) collective-permute-start(f32[2,512,512]{2,1,0:T(8,128)} %slice_select_fusion), channel_id=1, source_target_pairs={{0,4},{1,5},{2,6},{3,7},{4,0},{5,1},{6,2},{7,3},{8,12},{9,13},{10,... | collective-permute-start | bytes 6291464 | tf_op jit(solution)/shard_map/ppermute | solution.py:12
  373.6 1.3 copy-start.3
  374.9 2.2 copy-start.10
  374.9 2.2 copy-start.11
  375.1 22.1 %collective-permute-start.4 = (f32[2,512,256]{2,1,0:T(8,128)S(1)}, f32[2,512,256]{2,1,0:T(8,128)}, u32[]{:S(2)}, u32[]{:S(2)}) collective-permute-start(f32[2,512,256]{2,1,0:T(8,128)S(1)} %slice_select_fusion.1), channel_id=1, source_target_pairs={{0,2},{1,3},{2,0},{3,1},{4,6},{5,7},{6,4},{7,5},{8,10},{9,11},{10,... | collective-permute-start | bytes 3145736 | tf_op jit(solution)/shard_map/ppermute | solution.py:12
  377.1 5.2 copy-start.2
  379.2 17.9 %copy-start.4 = (f32[2,512,512]{2,1,0:T(8,128)S(1)}, f32[2,512,512]{2,1,0:T(8,128)}, u32[]{:S(2)}) copy-start(f32[2,512,512]{2,1,0:T(8,128)} %copy-done.3) | copy-start | bytes 6291460
  381.6 0.7 copy-start.7
  398.6 4.1 copy-start.8
  399.4 378.6 %collective-permute-start.5 = (f32[2,512,128]{2,1,0:T(8,128)}, f32[2,512,128]{2,1,0:T(8,128)}, u32[]{:S(2)}, u32[]{:S(2)}) collective-permute-start(f32[2,512,128]{2,1,0:T(8,128)} %slice_select_fusion.2), channel_id=1, source_target_pairs={{0,1},{1,0},{2,3},{3,2},{4,5},{5,4},{6,7},{7,6},{8,9},{9,8},{10,11... | collective-permute-start | bytes 1572872 | tf_op jit(solution)/shard_map/ppermute | solution.py:12
  776.9 92.5 %copy-start.9 = (bf16[1,2,512,128]{3,2,1,0:T(8,128)(2,1)S(1)}, bf16[1,2,512,128]{3,2,1,0:T(8,128)(2,1)}, u32[]{:S(2)}) copy-start(bf16[1,2,512,128]{3,2,1,0:T(8,128)(2,1)} %param.9) | copy-start | bytes 786436
  779.3 97.9 %collective-permute-start.6 = (bf16[2,512,128]{2,1,0:T(8,128)(2,1)S(1)}, bf16[2,512,128]{2,1,0:T(8,128)(2,1)S(1)}, u32[]{:S(2)}, u32[]{:S(2)}) collective-permute-start(bf16[2,512,128]{2,1,0:T(8,128)(2,1)S(1)} %fusion.6), channel_id=1, source_target_pairs={{64,0},{128,64},{192,128},{256,192},{320,256},{384,320},{448,384},... | collective-permute-start | bytes 786440 | tf_op jit(solution)/shard_map/ppermute | solution.py:18
where the time goes:
time: 878 us
  blocking collectives  647 us (74%)
  starting transfers between devices  119 us (14%)
  waiting for transfers between devices  80.5 us (9%)
  other arithmetic  16.1 us (2%)
  matrix products  9.77 us (1%)
    psum x1, blocking collectives, shards(): lowrank = lax.psum(padded_rank, 'tensor').astype(jnp.bfloat16)  374 us
    all_gather x1, blocking collectives, shards(): hidden = lax.all_gather(saved_rank_outputs[0], 'tensor', axis=1, tiled=True)  273 us
    ppermute x1, starting transfers between devices, shifted(): return lax.ppermute(block, axis, route)  90 us
    ppermute x6, waiting for transfers between devices, partner(): return lax.ppermute(value, axis, pairs)  74.1 us
    ppermute x6, starting transfers between devices, partner(): return lax.ppermute(value, axis, pairs)  28.8 us
  transfers between devices with their start and end apart: 7, of which 5 were waited for; matrix products, arithmetic and copies ran while one was open for 1% of the time, Pallas kernels for 0%

commit v1 on v0

--- a/solution.py
+++ b/solution.py
@@ -86,7 +86,7 @@
     padded_rank = lax.dynamic_update_slice_in_dim(
         padded_rank, partial_rank, high_index * rank_part, 3
     )
-    lowrank = lax.psum(padded_rank, "tensor").astype(jnp.bfloat16)
+    lowrank = jnp.sum(lax.all_gather(padded_rank, "tensor"), axis=0).astype(jnp.bfloat16)
     selected_down_matrix = choose_segment_rows(class_indicator, adapter_down_maps[0])
     adapter = jnp.einsum(
         "mskr,msrd->mskd", lowrank, selected_down_matrix, preferred_element_type=jnp.float32

time: 878 us -> 535 us (0.61)
  blocking collectives: 647 us -> 259 us
  waiting for transfers between devices: 80.5 us -> 122 us
  starting transfers between devices: 119 us -> 102 us
  between operations: 0.98 us -> 14.4 us
    psum x1 -> x0, blocking collectives: 374 us -> none  [shards(): lowrank = lax.psum(padded_rank, 'tensor').astype(jnp.bfloat16)]
    ppermute x1, starting transfers between devices: 90 us -> 23.9 us  [shifted(): return lax.ppermute(block, axis, route)]
    ppermute x6, starting transfers between devices: 28.8 us -> 78 us  [partner(): return lax.ppermute(value, axis, pairs)]
    ppermute x6, waiting for transfers between devices: 74.1 us -> 110 us  [partner(): return lax.ppermute(value, axis, pairs)]
    all_gather x1, blocking collectives: 273 us -> 259 us  [shards(): hidden = lax.all_gather(saved_rank_outputs[0], 'tensor', axis=1, tiled=True)]
  transfers between devices with their start and end apart: 7 -> 8, of which waited for: 5 -> 5; matrix products, arithmetic and copies ran while one was open for 1% -> 4% of each run, Pallas kernels for 0% -> 0%
where the time goes in v1:
time: 535 us; the launch traced here: 534 us
  blocking collectives  259 us (48%)
  waiting for transfers between devices  122 us (23%)
  starting transfers between devices  102 us (19%)
  other arithmetic  23.8 us (4%)
  between operations  14.4 us (3%)
  matrix products  7.11 us (1%)
  local copies, waits for them, and re-layouts  6.23 us (1%)
    all_gather x1, blocking collectives, shards(): hidden = lax.all_gather(saved_rank_outputs[0], 'tensor', axis=1, tiled=True)  259 us
    ppermute x6, waiting for transfers between devices, partner(): return lax.ppermute(value, axis, pairs)  110 us
    ppermute x6, starting transfers between devices, partner(): return lax.ppermute(value, axis, pairs)  78 us
    ppermute x1, starting transfers between devices, shifted(): return lax.ppermute(block, axis, route)  23.9 us
    ppermute x1, waiting for transfers between devices, shifted(): return lax.ppermute(block, axis, route)  11.5 us
  transfers between devices with their start and end apart: 8, of which 5 were waited for; matrix products, arithmetic and copies ran while one was open for 4% of the time, Pallas kernels for 0%

profile of v1, /device:TPU:9, one launch (start us, length us, event | category | flops | bytes accessed | tf_op | source)
XLA Modules:
  0.0 534.2 jit_solution(14032122340949293294)
XLA Ops:
  8.1 1.0 bitcast_select_fusion
  9.2 3.1 collective-permute-start
  12.3 6.0 %collective-permute-done = bf16[2,64,1024]{2,1,0:T(8,128)(2,1)S(1)} collective-permute-done((bf16[2,64,1024]{2,1,0:T(8,128)(2,1)S(1)}, bf16[2,64,1024]{2,1,0:T(8,128)(2,1)S(1)}, u32[]{:S(2)}, u32[]{:S(2)}) %collective-permute-start) | collective-permute-done | bytes 262176 | tf_op jit(solution)/shard_map/ppermute | solution.py:12
  18.4 4.7 collective-permute-start.1
  23.1 10.8 %collective-permute-done.1 = bf16[2,128,1024]{2,1,0:T(8,128)(2,1)} collective-permute-done((bf16[2,128,1024]{2,1,0:T(8,128)(2,1)S(1)}, bf16[2,128,1024]{2,1,0:T(8,128)(2,1)}, u32[]{:S(2)}, u32[]{:S(2)}) %collective-permute-start.1) | collective-permute-done | bytes 524320 | tf_op jit(solution)/shard_map/ppermute | solution.py:12
  33.9 2.0 maximum_select_fusion.1
  35.9 6.6 %collective-permute-start.2 = (bf16[2,256,1024]{2,1,0:T(8,128)(2,1)S(1)}, bf16[2,256,1024]{2,1,0:T(8,128)(2,1)}, u32[]{:S(2)}, u32[]{:S(2)}) collective-permute-start(bf16[2,256,1024]{2,1,0:T(8,128)(2,1)S(1)} %maximum_select_fusion.1), channel_id=1, source_target_pairs={{0,32},{1,33},{2,34},{3,35},{4,36},{5,37},{6,38},{7,39},{8,40},{9,... | collective-permute-start | bytes 3145736 | tf_op jit(solution)/shard_map/ppermute | solution.py:12
  42.7 42.7 %collective-permute-done.2 = bf16[2,256,1024]{2,1,0:T(8,128)(2,1)} collective-permute-done((bf16[2,256,1024]{2,1,0:T(8,128)(2,1)S(1)}, bf16[2,256,1024]{2,1,0:T(8,128)(2,1)}, u32[]{:S(2)}, u32[]{:S(2)}) %collective-permute-start.2) | collective-permute-done | bytes 1048608 | tf_op jit(solution)/shard_map/ppermute | solution.py:12
  85.4 2.5 maximum_select_fusion
  88.0 1.3 copy-done.1
  90.7 4.0 fusion
  94.7 2.2 slice_select_fusion
  97.5 10.6 %collective-permute-start.3 = (f32[2,512,512]{2,1,0:T(8,128)}, f32[2,512,512]{2,1,0:T(8,128)}, u32[]{:S(2)}, u32[]{:S(2)}) collective-permute-start(f32[2,512,512]{2,1,0:T(8,128)} %slice_select_fusion), channel_id=1, source_target_pairs={{0,4},{1,5},{2,6},{3,7},{4,0},{5,1},{6,2},{7,3},{8,12},{9,13},{10,... | collective-permute-start | bytes 6291464 | tf_op jit(solution)/shard_map/ppermute | solution.py:12
  108.1 50.7 %collective-permute-done.3 = f32[2,512,512]{2,1,0:T(8,128)} collective-permute-done((f32[2,512,512]{2,1,0:T(8,128)}, f32[2,512,512]{2,1,0:T(8,128)}, u32[]{:S(2)}, u32[]{:S(2)}) %collective-permute-start.3) | collective-permute-done | bytes 2097184 | tf_op jit(solution)/shard_map/ppermute | solution.py:12
  158.8 3.6 select_add_fusion
  162.5 1.3 copy-done.3
  163.9 51.1 %collective-permute-start.4 = (f32[2,512,256]{2,1,0:T(8,128)S(1)}, f32[2,512,256]{2,1,0:T(8,128)}, u32[]{:S(2)}, u32[]{:S(2)}) collective-permute-start(f32[2,512,256]{2,1,0:T(8,128)S(1)} %slice_select_fusion.1), channel_id=1, source_target_pairs={{0,2},{1,3},{2,0},{3,1},{4,6},{5,7},{6,4},{7,5},{8,10},{9,11},{10,... | collective-permute-start | bytes 3145736 | tf_op jit(solution)/shard_map/ppermute | solution.py:12
  215.1 259.1 %all-gather = bf16[1,2,512,64]{3,2,1,0:T(8,128)(2,1)S(1)} all-gather(bf16[1,2,8,64]{3,2,1,0:T(8,128)(2,1)S(1)} %copy-done.11), channel_id=2, replica_groups=mesh['pipe'=8,'tensor'=64] {'tensor'}, dimensions={2}, use_global_device_ids=true | all-gather | bytes 133120 | tf_op jit(solution)/shard_map/all_gather | solution.py:102
  474.6 2.2 select_add_fusion.1
  477.6 1.9 collective-permute-start.5
  481.3 7.0 %reduce_sum.9 = bf16[2,4,128,64]{2,3,1,0:T(8,128)(2,1)S(1)} reduce(f32[64,2,4,128,64]{3,4,2,1,0:T(8,128)} %all-gather.3.cloned.1.call-done, f32[]{:T(128)} %constant.48.clone.1), dimensions={0}, to_apply=%region_0.1 | reduce | flops 4128768 | bytes 16908292 | tf_op jit(solution)/shard_map/reduce_sum | solution.py:89
  488.6 1.2 fusion.7
  489.8 23.9 %collective-permute-start.6 = (bf16[2,512,128]{2,1,0:T(8,128)(2,1)S(1)}, bf16[2,512,128]{2,1,0:T(8,128)(2,1)S(1)}, u32[]{:S(2)}, u32[]{:S(2)}) collective-permute-start(bf16[2,512,128]{2,1,0:T(8,128)(2,1)S(1)} %fusion.7), channel_id=1, source_target_pairs={{64,0},{128,64},{192,128},{256,192},{320,256},{384,320},{448,384},... | collective-permute-start | bytes 786440 | tf_op jit(solution)/shard_map/ppermute | solution.py:18
  515.1 11.5 %collective-permute-done.6 = bf16[2,512,128]{2,1,0:T(8,128)(2,1)S(1)} collective-permute-done((bf16[2,512,128]{2,1,0:T(8,128)(2,1)S(1)}, bf16[2,512,128]{2,1,0:T(8,128)(2,1)S(1)}, u32[]{:S(2)}, u32[]{:S(2)}) %collective-permute-start.6) | collective-permute-done | bytes 262176 | tf_op jit(solution)/shard_map/ppermute | solution.py:18
  (45 shorter events, 8.8 us)
Async XLA Ops:
  7.2 83.6 %copy-start = (bf16[1,1,1024,1024]{3,2,1,0:T(8,128)(2,1)S(1)}, bf16[1,1,1024,1024]{3,2,1,0:T(8,128)(2,1)}, u32[]{:S(2)}) copy-start(bf16[1,1,1024,1024]{3,2,1,0:T(8,128)(2,1)} %param.11) | copy-start | bytes 6291460
  7.2 35.3 %copy-start.10 = (s32[1,2,4]{2,1,0:T(2,128)S(1)}, s32[1,2,4]{2,1,0:T(2,128)}, u32[]{:S(2)}) copy-start(s32[1,2,4]{2,1,0:T(2,128)} %param.14) | copy-start | bytes 100
  7.2 35.3 %copy-start.8 = (bf16[1,1,8,8,1024]{4,3,2,1,0:T(8,128)(2,1)S(1)}, bf16[1,1,8,8,1024]{4,3,2,1,0:T(8,128)(2,1)}, u32[]{:S(2)}) copy-start(bf16[1,1,8,8,1024]{4,3,2,1,0:T(8,128)(2,1)} %param.13) | copy-start | bytes 393220
  7.2 474.1 %all-gather.3.cloned.1.call-start = ((), (), s32[]{:S(2)}) async-start(), calls=%async_computation | async-start | bytes 17039360 | tf_op jit(solution)/shard_map/all_gather | solution.py:89
  9.2 9.1 %collective-permute-start = (bf16[2,64,1024]{2,1,0:T(8,128)(2,1)S(1)}, bf16[2,64,1024]{2,1,0:T(8,128)(2,1)S(1)}, u32[]{:S(2)}, u32[]{:S(2)}) collective-permute-start(bf16[2,64,1024]{2,1,0:T(8,128)(2,1)S(1)} %bitcast_select_fusion), channel_id=1, source_target_pairs={{0,8},{1,9},{2,10},{3,11},{4,12},{5,13},{6,14},{7,15},{8,0},{9,1},... | collective-permute-start | bytes 786440 | tf_op jit(solution)/shard_map/ppermute | solution.py:12
  18.4 4.7 copy-start.5
  18.4 15.5 %collective-permute-start.1 = (bf16[2,128,1024]{2,1,0:T(8,128)(2,1)S(1)}, bf16[2,128,1024]{2,1,0:T(8,128)(2,1)}, u32[]{:S(2)}, u32[]{:S(2)}) collective-permute-start(bf16[2,128,1024]{2,1,0:T(8,128)(2,1)S(1)} %maximum_select_fusion.2), channel_id=1, source_target_pairs={{0,16},{1,17},{2,18},{3,19},{4,20},{5,21},{6,22},{7,23},{8,24},{9,... | collective-permute-start | bytes 1572872 | tf_op jit(solution)/shard_map/ppermute | solution.py:12
  35.9 49.6 %collective-permute-start.2 = (bf16[2,256,1024]{2,1,0:T(8,128)(2,1)S(1)}, bf16[2,256,1024]{2,1,0:T(8,128)(2,1)}, u32[]{:S(2)}, u32[]{:S(2)}) collective-permute-start(bf16[2,256,1024]{2,1,0:T(8,128)(2,1)S(1)} %maximum_select_fusion.1), channel_id=1, source_target_pairs={{0,32},{1,33},{2,34},{3,35},{4,36},{5,37},{6,38},{7,39},{8,40},{9,... | collective-permute-start | bytes 3145736 | tf_op jit(solution)/shard_map/ppermute | solution.py:12
  88.0 1.4 copy-start.1
  90.0 0.7 copy-start.6
  94.7 2.7 copy-start.4
  97.5 61.4 %collective-permute-start.3 = (f32[2,512,512]{2,1,0:T(8,128)}, f32[2,512,512]{2,1,0:T(8,128)}, u32[]{:S(2)}, u32[]{:S(2)}) collective-permute-start(f32[2,512,512]{2,1,0:T(8,128)} %slice_select_fusion), channel_id=1, source_target_pairs={{0,4},{1,5},{2,6},{3,7},{4,0},{5,1},{6,2},{7,3},{8,12},{9,13},{10,... | collective-permute-start | bytes 6291464 | tf_op jit(solution)/shard_map/ppermute | solution.py:12
  162.5 1.3 copy-start.3
  163.8 51.3 %copy-start.11 = (bf16[1,2,8,64]{3,2,1,0:T(8,128)(2,1)S(1)}, bf16[1,2,8,64]{3,2,1,0:T(8,128)(2,1)}, u32[]{:S(2)}) copy-start(bf16[1,2,8,64]{3,2,1,0:T(8,128)(2,1)} %param.10) | copy-start | bytes 6148
  163.8 310.5 %copy-start.9 = (bf16[1,8,64,128]{3,2,1,0:T(8,128)(2,1)S(1)}, bf16[1,8,64,128]{3,2,1,0:T(8,128)(2,1)}, u32[]{:S(2)}) copy-start(bf16[1,8,64,128]{3,2,1,0:T(8,128)(2,1)} %param.12) | copy-start | bytes 393220
  163.9 310.6 %collective-permute-start.4 = (f32[2,512,256]{2,1,0:T(8,128)S(1)}, f32[2,512,256]{2,1,0:T(8,128)}, u32[]{:S(2)}, u32[]{:S(2)}) collective-permute-start(f32[2,512,256]{2,1,0:T(8,128)S(1)} %slice_select_fusion.1), channel_id=1, source_target_pairs={{0,2},{1,3},{2,0},{3,1},{4,6},{5,7},{6,4},{7,5},{8,10},{9,11},{10,... | collective-permute-start | bytes 3145736 | tf_op jit(solution)/shard_map/ppermute | solution.py:12
  474.5 5.0 copy-start.2
  477.6 11.0 %collective-permute-start.5 = (f32[2,512,128]{2,1,0:T(8,128)}, f32[2,512,128]{2,1,0:T(8,128)}, u32[]{:S(2)}, u32[]{:S(2)}) collective-permute-start(f32[2,512,128]{2,1,0:T(8,128)} %slice_select_fusion.2), channel_id=1, source_target_pairs={{0,1},{1,0},{2,3},{3,2},{4,5},{5,4},{6,7},{7,6},{8,9},{9,8},{10,11... | collective-permute-start | bytes 1572872 | tf_op jit(solution)/shard_map/ppermute | solution.py:12
  488.3 25.4 %copy-start.7 = (bf16[1,2,512,128]{3,2,1,0:T(8,128)(2,1)S(1)}, bf16[1,2,512,128]{3,2,1,0:T(8,128)(2,1)}, u32[]{:S(2)}) copy-start(bf16[1,2,512,128]{3,2,1,0:T(8,128)(2,1)} %param.9) | copy-start | bytes 786436
  489.8 36.9 %collective-permute-start.6 = (bf16[2,512,128]{2,1,0:T(8,128)(2,1)S(1)}, bf16[2,512,128]{2,1,0:T(8,128)(2,1)S(1)}, u32[]{:S(2)}, u32[]{:S(2)}) collective-permute-start(bf16[2,512,128]{2,1,0:T(8,128)(2,1)S(1)} %fusion.7), channel_id=1, source_target_pairs={{64,0},{128,64},{192,128},{256,192},{320,256},{384,320},{448,384},... | collective-permute-start | bytes 786440 | tf_op jit(solution)/shard_map/ppermute | solution.py:18
Sparse Core Ops, SparseCore 0:
  90.9 359.4 all-gather.2
